TPU v7x, 512 devices: a whole 4x8x8 slice. The times are simulated.
512 devices in a mesh: dp: 8 (over y), row: 4 (over z_lo), col: 16 (over x, z_hi, core).
Axes of the slice: x: 4, y: 8, z: 8 (z_hi: 2, z_lo: 4; z = z_hi * 4 + z_lo), core: 2. Of those that a mesh axis runs over, the one named last changes fastest.
Arguments:
- tokens: bfloat16 [2048, 4096], P(('dp', 'col'), 'row'), may hold values from -6 to 6
- gate_weight: bfloat16 [4096, 14336], P('row', 'col'), may hold values from -0.125 to 0.125
- up_weight: bfloat16 [4096, 14336], P('row', 'col'), may hold values from -0.125 to 0.125
- gate_mask: int32 [32, 112], P('row', 'col'), may hold values 0 or 1
- up_mask: int32 [32, 112], P('row', 'col'), may hold values 0 or 1
- slope: bfloat16 [2048, 14336], P(('dp', 'row'), 'col'), may hold values from -6 to 6
Outputs:
- hidden: bfloat16 [2048, 14336], P(('dp', 'row'), 'col')
- input_grad: bfloat16 [2048, 4096], P(('dp', 'col'), 'row')
- gate_grad: bfloat16 [32, 128, 14336], P('row', 'dp', 'col')
- up_grad: bfloat16 [32, 128, 14336], P('row', 'dp', 'col')
Inputs may be any that keep to these rules, and one draw needn't show every extreme that they name: `gate_mask`: 1 marks a live 128 x 128 block of the projection, 0 a pruned one. `up_mask`: 1 marks a live 128 x 128 block of the projection, 0 a pruned one.
All inputs are finite; a program needn't handle non-finite values.
Results may differ from a plain program's by a relative error of at most 0.0058.
Values may be sent and summed in bfloat16 or wider, within the bound.
No kernel may reach another device: no remote copies, remote signals or barrier semaphores. Data moves between devices by JAX's collectives and lax.ppermute only.
A program may use at most 64 MiB of HBM per device.

v0:
```python
import jax
import jax.numpy as jnp
from jax import lax
from jax.sharding import PartitionSpec as P


def expand_mask(mask, block, height):
    blocks_down, blocks_across = mask.shape
    grid = mask.astype(jnp.float32)[:, None, :, None]
    return jnp.broadcast_to(grid, (blocks_down, height, blocks_across, block)).reshape(
        blocks_down, height, blocks_across * block
    )


def body(tokens, gate_weight, up_weight, gate_mask, up_mask, slope):
    block = gate_weight.shape[0] // gate_mask.shape[0]
    width_part = gate_weight.shape[0]
    hidden_part = gate_weight.shape[1]
    gate_live = (
        gate_weight.astype(jnp.float32)
        * expand_mask(gate_mask, block, block).reshape(width_part, hidden_part)
    ).astype(jnp.bfloat16)
    up_live = (
        up_weight.astype(jnp.float32)
        * expand_mask(up_mask, block, block).reshape(width_part, hidden_part)
    ).astype(jnp.bfloat16)
    paired = jnp.concatenate([gate_live, up_live], axis=1)
    gathered = lax.all_gather(tokens, "col", axis=0, tiled=True)
    replica_tokens = gathered.shape[0]
    rows_here = gathered
    sums = lax.psum_scatter(
        jnp.dot(rows_here, paired, preferred_element_type=jnp.float32),
        "row",
        scatter_dimension=0,
        tiled=True,
    )
    gate = sums[:, :hidden_part]
    up = sums[:, hidden_part:]
    sigma = jax.nn.sigmoid(gate)
    act = gate * sigma
    hidden = (act * up).astype(jnp.bfloat16)
    slope_wide = slope.astype(jnp.float32)
    gate_slope = (slope_wide * up * sigma * (1.0 + gate * (1.0 - sigma))).astype(jnp.bfloat16)
    up_slope = (slope_wide * act).astype(jnp.bfloat16)
    slopes = jnp.concatenate([gate_slope, up_slope], axis=1)
    replica = lax.axis_index("dp")
    replicas = lax.axis_size("dp")
    share = block // replicas
    blocks_down = width_part // block
    everyone = lax.all_gather(slopes, ("dp", "row"), axis=0, tiled=True)
    local_slopes = lax.dynamic_slice_in_dim(everyone, replica * replica_tokens, replica_tokens, 0)
    by_owner = gathered.reshape(replica_tokens, blocks_down, replicas, share)
    by_owner = jnp.transpose(by_owner, (2, 0, 1, 3)).reshape(
        replicas, replica_tokens, blocks_down * share
    )
    feats = lax.all_to_all(by_owner, "dp", split_axis=0, concat_axis=0, tiled=True)
    partial_value = jnp.einsum(
        "ptk,ptf->pkf",
        feats,
        everyone.reshape(replicas, replica_tokens, -1),
        preferred_element_type=jnp.float32,
    )
    rounded = lax.optimization_barrier(partial_value.astype(jnp.bfloat16))
    grads = jnp.sum(rounded.astype(jnp.float32), axis=0).reshape(
        blocks_down, share, 2 * hidden_part
    )
    rows_here = local_slopes
    input_grad = lax.psum_scatter(
        lax.dot_general(
            rows_here, paired, (((1,), (1,)), ((), ())), preferred_element_type=jnp.float32
        ),
        "col",
        scatter_dimension=0,
        tiled=True,
    ).astype(jnp.bfloat16)
    gate_grad = (grads[:, :, :hidden_part] * expand_mask(gate_mask, block, share)).astype(
        jnp.bfloat16
    )
    up_grad = (grads[:, :, hidden_part:] * expand_mask(up_mask, block, share)).astype(jnp.bfloat16)
    return (hidden, input_grad, gate_grad, up_grad)


def solution(mesh):
    return jax.shard_map(
        body,
        mesh=mesh,
        in_specs=(
            P(("dp", "col"), "row"),
            P("row", "col"),
            P("row", "col"),
            P("row", "col"),
            P("row", "col"),
            P(("dp", "row"), "col"),
        ),
        out_specs=(
            P(("dp", "row"), "col"),
            P(("dp", "col"), "row"),
            P("row", "dp", "col"),
            P("row", "dp", "col"),
        ),
        check_vma=False,
    )
```

profile of v0, /device:TPU:8, one launch (start us, length us, event | category | flops | bytes accessed | tf_op | source)
XLA Modules:
  0.0 386.7 jit_solution(408374661671901712)
XLA Ops:
  7.2 39.3 %all_gather.6 = bf16[256,1024]{1,0:T(8,128)(2,1)S(1)} all-gather(bf16[16,1024]{1,0:T(8,128)(2,1)} %param.6), channel_id=1, replica_groups=mesh['dp'=8,'row'=4,'col'=16] {'col'}, dimensions={0}, use_global_device_ids=true | all-gather | bytes 557056 | tf_op jit(solution)/shard_map/all_gather | solution.py:28
  46.5 0.7 convert_element_type.54
  47.3 2.9 copy.44
  50.3 3.8 copy.42
  54.1 0.3 broadcast_in_dim.33
  54.4 0.3 broadcast_in_dim.32
  54.7 0.9 copy-done
  55.6 2.5 fusion
  58.1 1.2 copy-done.1
  59.3 0.6 copy-done.3
  59.9 1.2 convolution_bitcast_fusion
  61.1 1.7 copy.57
  63.0 0.8 copy.46
  63.8 43.9 %reduce-scatter.7.cloned.1.call-done = f32[64,1792]{1,0:T(8,128)} async-done(((f32[256,1792]{1,0:T(8,128)}), f32[64,1792]{1,0:T(8,128)}) %reduce-scatter.7.cloned.1.call-update) | async-done | bytes 458768
  107.7 1.1 fusion.15
  108.8 0.2 copy.60
  109.0 0.2 copy.59
  109.2 1.4 fusion.7
  110.6 0.1 pad_maximum_fusion.3
  110.7 0.9 copy.47
  111.6 0.2 copy.48
  111.8 1.0 copy.50
  112.8 7.3 %all-to-all-start = ((bf16[8,256,128]{2,1,0:T(8,128)(2,1)}), bf16[8,256,128]{2,1,0:T(8,128)(2,1)S(1)}, u32[]{:S(2)}, u32[]{:S(2)}) async-start(bf16[8,256,128]{2,1,0:T(8,128)(2,1)} %copy.50), calls=%async_computation.1 | async-start | bytes 1048576 | tf_op jit(solution)/shard_map/all_to_all | solution.py:56
  120.1 165.6 %all-gather.2.cloned.1.call-done = bf16[2048,1792]{1,0:T(8,128)(2,1)} async-done(((bf16[64,1792]{1,0:T(8,128)(2,1)}), bf16[2048,1792]{1,0:T(8,128)(2,1)}) %all-gather.2.cloned.1.call-update) | async-done | bytes 7340048 | tf_op jit(solution)/shard_map/all_gather | solution.py:50
  285.7 3.9 %fusion.3 = f32[256,1024]{1,0:T(8,128)} fusion(bf16[1024,896]{0,1:T(8,128)(2,1)S(1)} %copy-done.2, bf16[1024,896]{0,1:T(8,128)(2,1)} %copy-done.3, bf16[2048,1792]{1,0:T(8,128)(2,1)} %all-gather.2.cloned.1.call-done, s32[]{:T(128)S(6)} %select_n.3), kind=kOutput, calls=%fused_computation.9 | convolution fusion | flops 946864128 | bytes 5636100 | tf_op jit(solution)/shard_map/dot_general | solution.py:69
  289.7 0.8 copy.55
  290.5 5.5 %fusion.2 = bf16[8,128,1792]{1,2,0:T(8,128)(2,1)S(1)} fusion(bf16[8,256,1792]{2,1,0:T(8,128)(2,1)} %bitcast.36, bf16[8,256,128]{2,1,0:T(8,128)(2,1)S(1)} %all-to-all-done), kind=kOutput, calls=%fused_computation.7 | convolution fusion | flops 941359104 | bytes 11534336 | tf_op jit(solution)/shard_map/ptk,ptf->pkf/dot_general | solution.py:57
  296.0 0.5 convert_reduce_fusion
  296.5 0.3 copy.52
  296.9 0.8 fusion.9
  297.7 81.0 %reduce-scatter.5.cloned.1.call-done = f32[16,1024]{1,0:T(8,128)} async-done(((f32[256,1024]{1,0:T(8,128)}), f32[16,1024]{1,0:T(8,128)}) %reduce-scatter.5.cloned.1.call-update) | async-done | bytes 65552 | tf_op jit(solution)/shard_map/reduce_scatter | solution.py:68
  378.7 1.5 convert_element_type.60
  (21 shorter events, 0.4 us)
Async XLA Ops:
  7.2 43.0 %copy-start.5 = (s32[8,7]{1,0:T(8,128)S(1)}, s32[8,7]{1,0:T(8,128)}, u32[]{:S(2)}) copy-start(s32[8,7]{1,0:T(8,128)} %param.9) | copy-start | bytes 676
  7.2 100.5 %reduce-scatter.7.cloned.1.call-start = ((), (), s32[]{:S(2)}) async-start(), calls=%async_computation.5 | async-start | bytes 2293760
  54.1 1.5 copy-start
  58.1 1.2 copy-start.1
  58.1 1.8 copy-start.3
  61.1 1.8 copy-start.4
  62.9 222.8 %all-gather.2.cloned.1.call-start = ((), (), s32[]{:S(2)}) async-start(), calls=%async_computation.3 | async-start | bytes 7569408 | tf_op jit(solution)/shard_map/all_gather | solution.py:50
  109.2 176.5 %copy-start.2 = (bf16[1024,896]{0,1:T(8,128)(2,1)S(1)}, bf16[1024,896]{0,1:T(8,128)(2,1)}, u32[]{:S(2)}) copy-start(bf16[1024,896]{0,1:T(8,128)(2,1)} %copy-done.1) | copy-start | bytes 5505028
  112.8 177.7 %all-to-all-start = ((bf16[8,256,128]{2,1,0:T(8,128)(2,1)}), bf16[8,256,128]{2,1,0:T(8,128)(2,1)S(1)}, u32[]{:S(2)}, u32[]{:S(2)}) async-start(bf16[8,256,128]{2,1,0:T(8,128)(2,1)} %copy.50), calls=%async_computation.1 | async-start | bytes 1048576 | tf_op jit(solution)/shard_map/all_to_all | solution.py:56
  120.1 258.6 %reduce-scatter.5.cloned.1.call-start = ((), (), s32[]{:S(2)}) async-start(), calls=%async_computation.4 | async-start | bytes 1114112 | tf_op jit(solution)/shard_map/reduce_scatter | solution.py:68
Sparse Core Ops, SparseCore 0:
  63.0 44.6 reduce-scatter.6
  111.7 173.9 all-gather.1
  290.4 88.1 reduce-scatter.4
where the time goes:
time: 387 us
  waiting for transfers between devices  291 us (75%)
  blocking collectives  39.3 us (10%)
  local copies, waits for them, and re-layouts  17.5 us (5%)
  between operations  13.9 us (4%)
  matrix products  10.6 us (3%)
  other arithmetic  7.47 us (2%)
  starting transfers between devices  7.34 us (2%)
    all_gather x1, waiting for transfers between devices, body(): everyone = lax.all_gather(slopes, ('dp', 'row'), axis=0, tiled=True)  166 us
    reduce_scatter x1, waiting for transfers between devices, body(): lax.psum_scatter(lax.dot_general(rows_here, paired, (((1,), (1,)), ((), (...  81 us
    unnamed x4, waiting for transfers between devices  44 us
    all_gather x1, blocking collectives, body(): gathered = lax.all_gather(tokens, 'col', axis=0, tiled=True)  39.3 us
    unnamed x19, local copies, waits for them, and re-layouts  13.2 us
  transfers between devices with their start and end apart: 4, of which 3 were waited for; matrix products, arithmetic and copies ran while one was open for 4% of the time, Pallas kernels for 0%

commit v1 on v0

--- a/solution.py
+++ b/solution.py
@@ -25,7 +25,13 @@
         * expand_mask(up_mask, block, block).reshape(width_part, hidden_part)
     ).astype(jnp.bfloat16)
     paired = jnp.concatenate([gate_live, up_live], axis=1)
-    gathered = lax.all_gather(tokens, "col", axis=0, tiled=True)
+    line_up = []
+    for _ in range(lax.psum(1, axis_name="col")):
+        line_up.append(tokens)
+    gathered = jnp.concatenate(
+        lax.all_to_all(jnp.stack(line_up, axis=0), concat_axis=0, axis_name="col", split_axis=0),
+        axis=0,
+    )
     replica_tokens = gathered.shape[0]
     rows_here = gathered
     sums = lax.psum_scatter(

time: 387 us -> 372 us (0.961)
  blocking collectives: 39.3 us -> 0 us
  starting transfers between devices: 7.34 us -> 20.2 us
  local copies, waits for them, and re-layouts: 17.5 us -> 26 us
    all_gather x1 -> x0, blocking collectives: 39.3 us -> none  [body(): gathered = lax.all_gather(tokens, 'col', axis=0, tiled=True)]
    all_to_all x0 -> x1, starting transfers between devices: none -> 12.8 us  [body(): lax.all_to_all(jnp.stack(line_up, axis=0), concat_axis=0, axis_name='col'...]
    all_gather x1, waiting for transfers between devices: 166 us -> 157 us  [body(): everyone = lax.all_gather(slopes, ('dp', 'row'), axis=0, tiled=True)]
    another operation x0 -> x2, local copies, waits for them, and re-layouts: none -> 6.22 us  [the longest x1 4.6 us: body(): by_owner = gathered.reshape(replica_tokens, blocks_down, replicas, share)]
    unnamed x4, waiting for transfers between devices: 44 us -> 49 us
    transpose x1, local copies, waits for them, and re-layouts: 0.04 us -> 4.99 us  [body(): jnp.transpose(by_owner, (2, 0, 1, 3))]
    unnamed x19 -> x15, local copies, waits for them, and re-layouts: 13.2 us -> 10.7 us
  transfers between devices with their start and end apart: 4 -> 5, of which waited for: 3 -> 4; matrix products, arithmetic and copies ran while one was open for 4% -> 9% of each run, Pallas kernels for 0% -> 0%
where the time goes in v1:
time: 372 us; the launch traced here: 371 us
  waiting for transfers between devices  291 us (78%)
  local copies, waits for them, and re-layouts  26 us (7%)
  starting transfers between devices  20.2 us (5%)
  between operations  13.9 us (4%)
  matrix products  12.6 us (3%)
  other arithmetic  7.75 us (2%)
    all_gather x1, waiting for transfers between devices, body(): everyone = lax.all_gather(slopes, ('dp', 'row'), axis=0, tiled=True)  157 us
    reduce_scatter x1, waiting for transfers between devices, body(): lax.psum_scatter(lax.dot_general(rows_here, paired, (((1,), (1,)), ((), (...  82.7 us
    unnamed x4, waiting for transfers between devices  49 us
    all_to_all x1, starting transfers between devices, body(): lax.all_to_all(jnp.stack(line_up, axis=0), concat_axis=0, axis_name='col'...  12.8 us
    unnamed x15, local copies, waits for them, and re-layouts  10.7 us
  transfers between devices with their start and end apart: 5, of which 4 were waited for; matrix products, arithmetic and copies ran while one was open for 9% of the time, Pallas kernels for 0%

profile of v1, /device:TPU:8, one launch (start us, length us, event | category | flops | bytes accessed | tf_op | source)
XLA Modules:
  0.0 371.1 jit_solution(16951294824687486178)
XLA Ops:
  7.2 1.6 stack.2
  8.8 12.8 %all-to-all-start = ((bf16[16,16,1024]{2,1,0:T(8,128)(2,1)}), bf16[16,16,1024]{2,1,0:T(8,128)(2,1)S(1)}, u32[]{:S(2)}, u32[]{:S(2)}) async-start(bf16[16,16,1024]{2,1,0:T(8,128)(2,1)} %stack.2), calls=%async_computation | async-start | bytes 1048576 | tf_op jit(solution)/shard_map/all_to_all | solution.py:32
  21.7 0.7 convert_element_type.54
  22.5 2.9 copy.41
  25.5 3.8 %copy.39 = bf16[1024,896]{0,1:T(8,128)(2,1)} copy(bf16[1024,896]{1,0:T(8,128)(2,1)} %param.7) | data formatting | bytes 3670016 | tf_op args[1]
  29.3 0.3 broadcast_in_dim.33
  29.6 0.3 broadcast_in_dim.32
  29.9 0.9 copy-done
  30.8 3.8 %fusion = (bf16[1024,896]{0,1:T(8,128)(2,1)}, bf16[1024,896]{0,1:T(8,128)(2,1)}) fusion(f32[112,8,8,128]{3,2,1,0:T(8,128)S(1)} %bitcast.34, bf16[1024,896]{0,1:T(8,128)(2,1)S(1)} %copy.41, f32[112,8,8,128]{3,2,1,0:T(8,128)S(1)} %bitcast.35, bf16[1024,896]{0,1:T(8,128)(2,1)S(1)} %copy-done), kind=kLoop, calls=%fused_computation.3 | loop fusion | flops 5505024 | bytes 14680064 | tf_op jit(solution)/shard_map/convert_element_type | solution.py:26
  34.6 1.9 all-to-all-done
  36.5 3.2 convolution_bitcast_fusion
  39.7 1.7 copy.53
  41.6 0.2 copy.43
  41.7 49.0 %reduce-scatter.7.cloned.1.call-done = f32[64,1792]{1,0:T(8,128)} async-done(((f32[256,1792]{1,0:T(8,128)}), f32[64,1792]{1,0:T(8,128)}) %reduce-scatter.7.cloned.1.call-update) | async-done | bytes 458768
  90.7 1.1 fusion.15
  91.8 0.2 copy.56
  92.0 0.2 copy.55
  92.2 0.3 fusion.7
  92.7 0.9 copy.44
  93.6 4.6 %reshape_reshape.11 = bf16[256,8,8,16]{3,2,1,0:T(8,128)(2,1)} reshape(bf16[16,16,1024]{2,1,0:T(8,128)(2,1)S(1)} %all-to-all-done) | data formatting | bytes 1048576 | tf_op jit(solution)/shard_map/reshape;reshape | solution.py:58
  98.2 5.0 %copy.45 = bf16[8,256,8,16]{1,3,2,0:T(8,128)(2,1)S(1)} copy(bf16[8,256,8,16]{3,0,2,1:T(8,128)(2,1)} %bitcast.33) | data formatting | bytes 1048576 | tf_op jit(solution)/shard_map/transpose | solution.py:59
  103.2 1.0 copy.46
  104.2 7.3 %all-to-all-start.1 = ((bf16[8,256,128]{2,1,0:T(8,128)(2,1)}), bf16[8,256,128]{2,1,0:T(8,128)(2,1)S(1)}, u32[]{:S(2)}, u32[]{:S(2)}) async-start(bf16[8,256,128]{2,1,0:T(8,128)(2,1)} %copy.46), calls=%async_computation.2 | async-start | bytes 1048576 | tf_op jit(solution)/shard_map/all_to_all | solution.py:62
  111.5 157.0 %all-gather.2.cloned.1.call-done = bf16[2048,1792]{1,0:T(8,128)(2,1)} async-done(((bf16[64,1792]{1,0:T(8,128)(2,1)}), bf16[2048,1792]{1,0:T(8,128)(2,1)}) %all-gather.2.cloned.1.call-update) | async-done | bytes 7340048 | tf_op jit(solution)/shard_map/all_gather | solution.py:56
  268.4 3.9 %fusion.3 = f32[256,1024]{1,0:T(8,128)} fusion(bf16[1024,896]{0,1:T(8,128)(2,1)S(1)} %copy-done.1, bf16[1024,896]{0,1:T(8,128)(2,1)} %get-tuple-element.28, bf16[2048,1792]{1,0:T(8,128)(2,1)} %all-gather.2.cloned.1.call-done, s32[]{:T(128)S(6)} %select_n.3), kind=kOutput, calls=%fused_computation.9 | convolution fusion | flops 946864128 | bytes 5636100 | tf_op jit(solution)/shard_map/dot_general | solution.py:75
  272.4 0.8 copy.51
  273.2 5.5 %fusion.2 = bf16[8,128,1792]{1,2,0:T(8,128)(2,1)S(1)} fusion(bf16[8,256,1792]{2,1,0:T(8,128)(2,1)} %bitcast.36, bf16[8,256,128]{2,1,0:T(8,128)(2,1)S(1)} %all-to-all-done.1), kind=kOutput, calls=%fused_computation.7 | convolution fusion | flops 941359104 | bytes 11534336 | tf_op jit(solution)/shard_map/ptk,ptf->pkf/dot_general | solution.py:63
  278.7 0.5 convert_reduce_fusion
  279.3 0.3 copy.48
  279.6 0.8 fusion.9
  280.4 82.7 %reduce-scatter.5.cloned.1.call-done = f32[16,1024]{1,0:T(8,128)} async-done(((f32[256,1024]{1,0:T(8,128)}), f32[16,1024]{1,0:T(8,128)}) %reduce-scatter.5.cloned.1.call-update) | async-done | bytes 65552 | tf_op jit(solution)/shard_map/reduce_scatter | solution.py:74
  363.1 1.5 convert_element_type.60
  (19 shorter events, 0.5 us)
Async XLA Ops:
  7.2 18.2 %copy-start.3 = (s32[8,7]{1,0:T(8,128)S(1)}, s32[8,7]{1,0:T(8,128)}, u32[]{:S(2)}) copy-start(s32[8,7]{1,0:T(8,128)} %param.9) | copy-start | bytes 676
  8.8 27.7 %all-to-all-start = ((bf16[16,16,1024]{2,1,0:T(8,128)(2,1)}), bf16[16,16,1024]{2,1,0:T(8,128)(2,1)S(1)}, u32[]{:S(2)}, u32[]{:S(2)}) async-start(bf16[16,16,1024]{2,1,0:T(8,128)(2,1)} %stack.2), calls=%async_computation | async-start | bytes 1048576 | tf_op jit(solution)/shard_map/all_to_all | solution.py:32
  21.7 69.1 %reduce-scatter.7.cloned.1.call-start = ((), (), s32[]{:S(2)}) async-start(), calls=%async_computation.6 | async-start | bytes 2293760
  29.3 1.5 copy-start
  39.7 1.8 copy-start.2
  41.5 226.9 %all-gather.2.cloned.1.call-start = ((), (), s32[]{:S(2)}) async-start(), calls=%async_computation.4 | async-start | bytes 7569408 | tf_op jit(solution)/shard_map/all_gather | solution.py:56
  98.2 170.3 %copy-start.1 = (bf16[1024,896]{0,1:T(8,128)(2,1)S(1)}, bf16[1024,896]{0,1:T(8,128)(2,1)}, u32[]{:S(2)}) copy-start(bf16[1024,896]{0,1:T(8,128)(2,1)} %get-tuple-element.27) | copy-start | bytes 5505028
  104.2 169.0 %all-to-all-start.1 = ((bf16[8,256,128]{2,1,0:T(8,128)(2,1)}), bf16[8,256,128]{2,1,0:T(8,128)(2,1)S(1)}, u32[]{:S(2)}, u32[]{:S(2)}) async-start(bf16[8,256,128]{2,1,0:T(8,128)(2,1)} %copy.46), calls=%async_computation.2 | async-start | bytes 1048576 | tf_op jit(solution)/shard_map/all_to_all | solution.py:62
  111.5 251.7 %reduce-scatter.5.cloned.1.call-start = ((), (), s32[]{:S(2)}) async-start(), calls=%async_computation.5 | async-start | bytes 1114112 | tf_op jit(solution)/shard_map/reduce_scatter | solution.py:74
Sparse Core Ops, SparseCore 0:
  41.6 49.0 reduce-scatter.6
  93.7 174.6 all-gather.1
  273.1 89.9 reduce-scatter.4
